TPU v7x, 32 devices: a whole 2x2x4 slice. The times are simulated.
32 devices in a mesh: row: 8 (over z, y), col: 4 (over x, core).
Axes of the slice: x: 2, y: 2, z: 4, core: 2. Of those that a mesh axis runs over, the one named last changes fastest.
Arguments:
- tokens_in: bfloat16 [192, 8192], P('row', 'col'), may hold values from -6 to 6
- gate_weight: bfloat16 [8192, 28672], P('col', 'row'), may hold values from -0.0625 to 0.0625
- up_weight: bfloat16 [8192, 28672], P('col', 'row'), may hold values from -0.0625 to 0.0625
- down_weight: bfloat16 [28672, 8192], P('row', 'col'), may hold values from -0.03125 to 0.03125
- out_grad: bfloat16 [192, 8192], P('row', 'col'), may hold values from -0.29882812 to 0.29882812
Outputs:
- output: bfloat16 [192, 8192], P('row', 'col')
- in_grad: bfloat16 [192, 8192], P('row', 'col')
- gate_grad: bfloat16 [8192, 28672], P('col', 'row')
- up_grad: bfloat16 [8192, 28672], P('col', 'row')
- down_grad: bfloat16 [28672, 8192], P('row', 'col')
All inputs are finite; a program needn't handle non-finite values.
Results may differ from a plain program's by a relative error of at most 0.0051.
Values may be sent and summed in bfloat16 or wider, within the bound.
A program may use at most 192 MiB of HBM per device.

v0:
```python
import functools

import jax
import jax.numpy as jnp
from jax import lax
from jax.experimental import pallas as pl
from jax.experimental.pallas import tpu as pltpu
from jax.sharding import PartitionSpec as P

BF16 = jnp.bfloat16


def contract_last(left, right):
    return lax.dot_general(
        left, right, (((1,), (1,)), ((), ())), preferred_element_type=jnp.float32
    )


def contract_first(left, right):
    return lax.dot_general(
        left, right, (((0,), (0,)), ((), ())), preferred_element_type=jnp.float32
    )


def contract_mid(left, right):
    return jnp.dot(left, right, preferred_element_type=jnp.float32)


def tile_of(size, most):
    best = size
    for tile in range(128, most + 1, 128):
        if size % tile == 0:
            best = tile
    return best


def weight_grad_kernel(left_ref, right_ref, out_ref):
    out_ref[...] = jnp.dot(
        left_ref[...], right_ref[...], preferred_element_type=jnp.float32
    ).astype(out_ref.dtype)


def weight_grad(left_t, right):
    rows, tokens = left_t.shape
    cols = right.shape[1]
    tile = tile_of(cols, 256)
    return pl.pallas_call(
        weight_grad_kernel,
        grid=(cols // tile,),
        in_specs=[
            pl.BlockSpec((rows, tokens), lambda i: (0, 0)),
            pl.BlockSpec((tokens, tile), lambda i: (0, i)),
        ],
        out_specs=pl.BlockSpec((rows, tile), lambda i: (0, i)),
        out_shape=jax.ShapeDtypeStruct((rows, cols), BF16),
        cost_estimate=pl.CostEstimate(
            flops=2 * tokens * rows * cols,
            bytes_accessed=2 * (tokens * rows + tokens * cols + rows * cols),
            transcendentals=0,
        ),
    )(left_t, right)


def gather_kernel(n_z, n_y, cores, *refs):
    count = (len(refs) - 7) // 2
    ins, outs = refs[:count], refs[count : 2 * count]
    own_sem, up_send, up_recv, down_send, down_recv, y_send, y_recv = refs[2 * count :]
    row = lax.axis_index("row")
    core = lax.rem(lax.axis_index("col"), cores)
    z, y = row // n_y, lax.rem(row, n_y)
    peers = [lax.rem(y + step, n_y) for step in range(1, n_y)]
    barrier = pltpu.get_barrier_semaphore()

    def greet(z_to, y_to):
        pl.semaphore_signal(
            barrier, inc=1, device_id={"row": z_to * n_y + y_to}, device_id_type=pl.DeviceIdType.MESH
        )

    @pl.when(z < n_z - 1)
    def _():
        greet(z + 1, y)

    @pl.when(z > 0)
    def _():
        greet(z - 1, y)

    for peer in peers:
        greet(z, peer)

    ends = jnp.where(z > 0, 1, 0) + jnp.where(z < n_z - 1, 1, 0)
    pl.semaphore_wait(barrier, ends + len(peers))

    def slot(z_of, y_of):
        return lax.rem(y_of + core * (n_y // 2), n_y) * n_z + z_of

    def copy(item, source, z_of, sems, z_to, y_to):
        target = outs[item].at[slot(z_of, y)]
        return pltpu.make_async_remote_copy(
            src_ref=target if source is None else source,
            dst_ref=target,
            send_sem=sems[0],
            recv_sem=sems[1],
            device_id={"row": z_to * n_y + y_to},
            device_id_type=pl.DeviceIdType.MESH,
        )

    def up(item, step):
        source = ins[item] if step == 0 else None
        sems = (up_send.at[item, step], up_recv.at[item, step])
        return copy(item, source, z - step, sems, z + 1, y)

    def down(item, step):
        source = ins[item] if step == 0 else None
        sems = (down_send.at[item, step], down_recv.at[item, step])
        return copy(item, source, z + step, sems, z - 1, y)

    def across(item, offset, z_of, own):
        source = ins[item] if own else None
        place = lax.rem(z_of + n_z, n_z)
        sems = (y_send.at[item, offset, place], y_recv.at[item, offset, place])
        return copy(item, source, z_of, sems, z, peers[offset])

    def sends(item, step, act):
        @pl.when((z < n_z - 1) & (z >= step))
        def _():
            act(up(item, step))

        @pl.when((z > 0) & (z + step <= n_z - 1))
        def _():
            act(down(item, step))

        for offset in range(n_y - 1):
            if step == 0:
                act(across(item, offset, z, True))
            else:

                @pl.when(z >= step)
                def _():
                    act(across(item, offset, z - step, False))

                @pl.when(z + step <= n_z - 1)
                def _():
                    act(across(item, offset, z + step, False))

    local = [
        pltpu.make_async_copy(ins[item], outs[item].at[slot(z, y)], own_sem.at[item])
        for item in range(count)
    ]
    for item in range(count):
        sends(item, 0, lambda c: c.start())
        local[item].start()
    for item in range(count):
        for step in range(1, n_z):

            @pl.when(z >= step)
            def _():
                up(item, step - 1).wait_recv()

            @pl.when(z + step <= n_z - 1)
            def _():
                down(item, step - 1).wait_recv()

            sends(item, step, lambda c: c.start())
    for item in range(count):
        local[item].wait()
        for offset in range(n_y - 1):
            for z_of in range(n_z):
                across(item, offset, z_of, False).wait_recv()
        for step in range(n_z):
            sends(item, step, lambda c: c.wait_send())


def gather_rows(n_z, n_y, cores, call, *arrays):
    count = len(arrays)
    line = pltpu.SemaphoreType.DMA((count, n_z))
    side = pltpu.SemaphoreType.DMA((count, n_y, n_z))
    shape = arrays[0].shape
    out = pl.pallas_call(
        functools.partial(gather_kernel, n_z, n_y, cores),
        out_shape=[jax.ShapeDtypeStruct((n_z * n_y,) + shape, a.dtype) for a in arrays],
        in_specs=[pl.BlockSpec(memory_space=pl.ANY)] * count,
        out_specs=[pl.BlockSpec(memory_space=pl.ANY)] * count,
        scratch_shapes=[pltpu.SemaphoreType.DMA((count,)), line, line, line, line, side, side],
        cost_estimate=pl.CostEstimate(
            flops=0, bytes_accessed=8 * n_z * n_y * count * arrays[0].size, transcendentals=0
        ),
        compiler_params=pltpu.CompilerParams(collective_id=call, has_side_effects=True),
    )(*arrays)
    return [value.reshape(-1, shape[1]) for value in out]


def make_shards(n_row, n_col):
    cores = 2 if n_col % 2 == 0 else 1
    n_x = n_col // cores
    n_y = n_x if n_row % n_x == 0 and n_x % 2 == 0 else (2 if n_row % 2 == 0 else 1)
    n_z = n_row // n_y
    half = cores == 2 and n_y % 2 == 0

    def row_swap(value, bit):
        return lax.ppermute(value, "row", [(r, r ^ bit) for r in range(n_row)])

    def x_move(value, step):
        pairs = [
            (x * cores + k, (x + step) % n_x * cores + k) for x in range(n_x) for k in range(cores)
        ]
        return lax.ppermute(value, "col", pairs)

    def core_move(value):
        pairs = [(x * cores + k, x * cores + 1 - k) for x in range(n_x) for k in range(cores)]
        return lax.ppermute(value, "col", pairs)

    def scatter_start(total, bit):
        row = lax.axis_index("row")
        core = lax.rem(lax.axis_index("col"), cores)
        z, y = row // n_y, lax.rem(row, n_y)
        slot = lax.rem(y + core * (n_y // 2), n_y) * n_z + z
        rows = total.shape[0] // 2
        side = (slot // bit) % 2
        keep = lax.dynamic_slice_in_dim(total, side * rows, rows)
        send = lax.dynamic_slice_in_dim(total, (1 - side) * rows, rows).astype(BF16)
        return keep, row_swap(send, bit // n_z if bit >= n_z else bit * n_y)

    def gather_step(value, bit):
        arrived = row_swap(value, bit // n_z if bit >= n_z else bit * n_y)

        def both(arrived):
            row = lax.axis_index("row")
            core = lax.rem(lax.axis_index("col"), cores)
            slot = lax.rem(lax.rem(row, n_y) + core * (n_y // 2), n_y) * n_z + row // n_y
            lower = (slot // bit) % 2 == 0
            return jnp.concatenate(
                [jnp.where(lower, value, arrived), jnp.where(lower, arrived, value)], axis=0
            )

        return arrived, both

    def scatter_until(total, bit, last):
        while True:
            keep, arrived = scatter_start(total, bit)
            if bit == last:
                return keep, arrived
            total = keep + arrived.astype(jnp.float32)
            bit //= 2

    def sum_core(part, dtype):
        if cores == 1:
            return part
        if half:
            rows = part.shape[0] // 2
            return part[:rows] + core_move(part[rows:].astype(dtype)).astype(jnp.float32)
        return part + core_move(part)

    def send_x(mine):
        return [x_move(mine, step) for step in range(1, n_x)]

    def add_all(mine, moved):
        for value in moved:
            mine = mine + value.astype(jnp.float32)
        return mine

    def join(share, moved):
        return share if moved is None else jnp.concatenate([share, moved], axis=0)

    def core_send(share):
        return core_move(share) if half else None

    tie = lax.optimization_barrier

    def shards(tokens_in, gate_weight, up_weight, down_weight, out_grad):
        (inputs_all,) = gather_rows(n_z, n_y, cores, 0, tokens_in)
        inputs_all, out_grad = tie((inputs_all, out_grad))
        arrived, both = gather_step(out_grad, 1)
        gate_part = contract_mid(inputs_all, gate_weight)
        inputs_all, gate_part, arrived = tie((inputs_all, gate_part, arrived))
        grad_all, bit = both(arrived), 2
        arrived, both = gather_step(grad_all, bit)
        gate_mine = sum_core(gate_part, BF16)
        gate_moved = send_x(gate_mine.astype(BF16))
        up_mine = sum_core(contract_mid(inputs_all, up_weight), jnp.float32)
        arrived, up_sent = tie((arrived, up_mine.astype(BF16)))
        up_moved = send_x(up_sent)
        grad_all = both(arrived)
        while bit < n_row // 2:
            bit *= 2
            arrived, both = gather_step(grad_all, bit)
            grad_all = both(arrived)
        d_part = contract_last(grad_all, down_weight)
        d_mine = sum_core(d_part, jnp.float32)
        d_sent, gate_moved, up_moved, inputs_t = tie(
            (d_mine.astype(BF16), gate_moved, up_moved, inputs_all.T)
        )
        d_moved = send_x(d_sent)
        gate_pre, up_pre = add_all(gate_mine, gate_moved), add_all(up_mine, up_moved)
        sigma = jax.nn.sigmoid(gate_pre)
        activated = gate_pre * sigma
        share = (activated * up_pre).astype(BF16)
        hidden = join(share, core_send(share))
        output_part = contract_mid(hidden, down_weight)
        d_moved, output_part = tie((d_moved, output_part))
        out_keep, out_moved = scatter_until(output_part, n_row // 2, max(n_z, 1))
        d_hidden = add_all(d_mine, d_moved)
        d_gate = (d_hidden * up_pre * sigma * (1.0 + gate_pre * (1.0 - sigma))).astype(BF16)
        d_up = (d_hidden * activated).astype(BF16)
        d_gate, d_up, hidden = tie((d_gate, d_up, hidden))
        d_gate_moved, d_up_moved = core_send(d_gate), core_send(d_up)
        down_grad = contract_first(hidden, grad_all).astype(BF16)
        d_gate_moved, d_up_moved, out_moved, down_grad = tie(
            (d_gate_moved, d_up_moved, out_moved, down_grad)
        )
        d_gate, d_up = join(d_gate, d_gate_moved), join(d_up, d_up_moved)
        out_part = out_keep + out_moved.astype(jnp.float32)
        out_keep, out_moved = scatter_until(out_part, n_z // 2, 2)
        in_part = contract_last(d_gate, gate_weight)
        in_part, out_moved, d_up = tie((in_part, out_moved, d_up))
        out_keep, out_moved = scatter_start(out_keep + out_moved.astype(jnp.float32), 1)
        in_part = in_part + contract_last(d_up, up_weight)
        in_part, d_gate, d_up, out_moved = tie((in_part, d_gate, d_up, out_moved))
        output = (out_keep + out_moved.astype(jnp.float32)).astype(BF16)
        in_keep, in_moved = scatter_until(in_part, n_row // 2, max(n_z, 1))
        gate_grad = weight_grad(inputs_t, d_gate)
        gate_grad, in_moved, d_up = tie((gate_grad, in_moved, d_up))
        in_keep, in_moved = scatter_until(in_keep + in_moved.astype(jnp.float32), n_z // 2, 2)
        up_grad = weight_grad(inputs_t, d_up)
        up_grad, in_moved = tie((up_grad, in_moved))
        in_keep, in_moved = scatter_start(in_keep + in_moved.astype(jnp.float32), 1)
        in_grad = (in_keep + in_moved.astype(jnp.float32)).astype(BF16)
        return (output, in_grad, gate_grad, up_grad, down_grad)

    return shards


def solution(mesh):
    in_specs = (P("row", "col"), P("col", "row"), P("col", "row"), P("row", "col"), P("row", "col"))
    out_specs = (
        P("row", "col"),
        P("row", "col"),
        P("col", "row"),
        P("col", "row"),
        P("row", "col"),
    )
    shards = make_shards(mesh.shape["row"], mesh.shape["col"])
    return jax.shard_map(shards, mesh=mesh, in_specs=in_specs, out_specs=out_specs, check_vma=False)
```

profile of v0, /device:TPU:0, one launch (start us, length us, event | category | flops | bytes accessed | tf_op | source)
XLA Modules:
  0.0 196.2 jit_solution(7644752782897804563)
XLA Ops:
  0.6 20.2 %shard_map.92 = bf16[8,24,2048]{2,1,0:T(8,128)(2,1)} custom-call(bf16[24,2048]{1,0:T(8,128)(2,1)} %refs_0_.1), custom_call_target="tpu_custom_call" | custom-call | bytes 3145728 | tf_op jit(solution)/shard_map/pallas_call | solution.py:178
  20.8 0.0 copy-start.21
  20.9 0.1 collective-permute-start
  20.9 10.1 %fusion.8 = f32[192,3584]{1,0:T(8,128)} fusion(bf16[192,2048]{1,0:T(8,128)(2,1)} %bitcast.15, bf16[2048,3584]{1,0:T(8,128)(2,1)} %param.6), kind=kOutput, calls=%fused_computation.45 | convolution fusion | flops 2818572288 | bytes 18219008 | tf_op jit(solution)/shard_map/dot_general | solution.py:26
  31.0 0.0 collective-permute-done
  31.1 3.1 %fusion.9 = f32[192,3584]{1,0:T(8,128)S(1)} fusion(bf16[192,2048]{1,0:T(8,128)(2,1)S(1)} %bitcast.17, bf16[2048,3584]{1,0:T(8,128)(2,1)S(1)} %copy-done.21), kind=kOutput, calls=%fused_computation.46 | convolution fusion | flops 2818572288 | bytes 18219008 | tf_op jit(solution)/shard_map/dot_general | solution.py:26
  34.1 0.0 copy-start
  34.1 0.0 copy-start.20
  34.1 0.1 slice.26
  34.2 1.4 copy-done
  35.7 0.0 collective-permute-start.2
  35.7 2.9 %collective-permute-start.1 = (bf16[48,2048]{1,0:T(8,128)(2,1)S(1)}, bf16[48,2048]{1,0:T(8,128)(2,1)S(1)}, u32[]{:S(2)}, u32[]{:S(2)}) collective-permute-start(bf16[48,2048]{1,0:T(8,128)(2,1)S(1)} %pad_maximum_fusion.6), channel_id=1, source_target_pairs={{0,16},{4,20},{8,24},{12,28},{16,0},{20,4},{24,8},{28,12},{1,17},{... | collective-permute-start | bytes 589832 | tf_op jit(solution)/shard_map/ppermute | solution.py:200
  38.7 0.1 collective-permute-done.2
  38.8 2.3 %fusion.5 = bf16[96,3584]{1,0:T(8,128)(2,1)} fusion(f32[96,3584]{1,0:T(8,128)S(1)} %collective-permute-done.2, f32[192,3584]{1,0:T(8,128)} %copy-done), kind=kLoop, calls=%fused_computation.42 | loop fusion | flops 688128 | bytes 3440640 | tf_op jit(solution)/shard_map/convert_element_type | solution.py:280
  41.1 7.3 %collective-permute-done.1 = bf16[48,2048]{1,0:T(8,128)(2,1)S(1)} collective-permute-done((bf16[48,2048]{1,0:T(8,128)(2,1)S(1)}, bf16[48,2048]{1,0:T(8,128)(2,1)S(1)}, u32[]{:S(2)}, u32[]{:S(2)}) %collective-permute-start.1) | collective-permute-done | bytes 196640 | tf_op jit(solution)/shard_map/ppermute | solution.py:200
  48.4 0.1 broadcast_select_fusion.3
  48.6 1.4 collective-permute-start.3
  49.9 2.3 %slice.56 = bf16[96,3584]{1,0:T(8,128)(2,1)} slice(f32[192,3584]{1,0:T(8,128)} %fusion.8), slice={[96:192], [0:3584]} | slice | bytes 1376256 | tf_op jit(solution)/shard_map/slice | solution.py:250
  52.2 7.3 %collective-permute-done.3 = bf16[96,2048]{1,0:T(8,128)(2,1)S(1)} collective-permute-done((bf16[96,2048]{1,0:T(8,128)(2,1)S(1)}, bf16[96,2048]{1,0:T(8,128)(2,1)S(1)}, u32[]{:S(2)}, u32[]{:S(2)}) %collective-permute-start.3) | collective-permute-done | bytes 393248 | tf_op jit(solution)/shard_map/ppermute | solution.py:200
  59.5 0.1 broadcast_select_fusion.1
  59.7 8.5 %fusion.1 = f32[192,3584]{1,0:T(8,128)S(1)} fusion(bf16[3584,2048]{1,0:T(8,128)(2,1)} %param.8, bf16[96,2048]{1,0:T(8,128)(2,1)S(1)} %get-tuple-element.72, bf16[96,2048]{1,0:T(8,128)(2,1)S(1)} %get-tuple-element.71), kind=kOutput, calls=%fused_computation.20 | convolution fusion | flops 2820145152 | bytes 18219008 | tf_op jit(solution)/shard_map/dot_general | solution.py:14
  68.2 0.0 copy-start.5
  68.3 1.3 slice.28
  69.6 0.6 copy-done.5
  70.2 2.2 %copy.11 = bf16[192,2048]{0,1:T(8,128)(2,1)} copy(bf16[192,2048]{1,0:T(8,128)(2,1)} %bitcast.16) | data formatting | bytes 1572864 | tf_op jit(solution)/shard_map/optimization_barrier | solution.py:274
  72.5 1.6 fusion.2
  74.1 0.0 copy-start.1
  74.1 1.6 collective-permute-start.6
  75.7 0.5 collective-permute-start.7
  76.2 2.3 %fusion.6 = bf16[96,3584]{1,0:T(8,128)(2,1)} fusion(f32[96,3584]{1,0:T(8,128)S(1)} %collective-permute-done.4, f32[192,3584]{1,0:T(8,128)} %copy-done.5), kind=kLoop, calls=%fused_computation.43 | loop fusion | flops 688128 | bytes 3440640 | tf_op jit(solution)/shard_map/convert_element_type | solution.py:290
  78.5 14.0 %collective-permute-done.6 = bf16[96,3584]{1,0:T(8,128)(2,1)S(1)} collective-permute-done((bf16[96,3584]{1,0:T(8,128)(2,1)S(1)}, bf16[96,3584]{1,0:T(8,128)(2,1)S(1)}, u32[]{:S(2)}, u32[]{:S(2)}) %collective-permute-start.6) | collective-permute-done | bytes 688160 | tf_op jit(solution)/shard_map/ppermute | solution.py:206
  92.5 14.3 %collective-permute-done.7 = bf16[96,3584]{1,0:T(8,128)(2,1)S(1)} collective-permute-done((bf16[96,3584]{1,0:T(8,128)(2,1)S(1)}, bf16[96,3584]{1,0:T(8,128)(2,1)S(1)}, u32[]{:S(2)}, u32[]{:S(2)}) %collective-permute-start.7) | collective-permute-done | bytes 688160 | tf_op jit(solution)/shard_map/ppermute | solution.py:206
  106.8 1.6 multiply_convert_fusion.2
  108.4 1.6 collective-permute-start.8
  109.9 0.9 collective-permute-done.9
  110.8 7.3 %fusion.7 = f32[192,2048]{1,0:T(8,128)S(1)} fusion(bf16[3584,2048]{1,0:T(8,128)(2,1)} %param.8, bf16[96,3584]{1,0:T(8,128)(2,1)} %collective-permute-done.9, bf16[96,3584]{1,0:T(8,128)(2,1)} %multiply_convert_fusion.2), kind=kOutput, calls=%fused_computation.44 | convolution fusion | flops 2821324800 | bytes 17629184 | tf_op jit(solution)/shard_map/dot_general | solution.py:26
  118.2 0.0 copy-start.2
  118.2 8.2 %collective-permute-done.8 = bf16[96,3584]{1,0:T(8,128)(2,1)S(1)} collective-permute-done((bf16[96,3584]{1,0:T(8,128)(2,1)}, bf16[96,3584]{1,0:T(8,128)(2,1)S(1)}, u32[]{:S(2)}, u32[]{:S(2)}) %collective-permute-start.8) | collective-permute-done | bytes 688160 | tf_op jit(solution)/shard_map/ppermute | solution.py:206
  126.4 1.4 pad_maximum_fusion
  127.8 2.1 %multiply_convert_fusion = (bf16[96,3584]{1,0:T(8,128)(2,1)}, bf16[96,3584]{1,0:T(8,128)(2,1)}) fusion(bf16[96,3584]{1,0:T(8,128)(2,1)S(1)} %collective-permute-done.8, f32[96,3584]{1,0:T(8,128)S(1)} %collective-permute-done.4, f32[192,3584]{1,0:T(8,128)S(1)} %copy-done.6, bf16[96,3584]{1,0:T(8,128)(2,1)S(1)} %copy-done.11, ...), kind=kLoop, calls=%fused_computation.6 | loop fusion | flops 7913472 | bytes 11010048 | tf_op jit(solution)/shard_map/convert_element_type | solution.py:303
  130.0 1.1 collective-permute-start.12
  131.2 0.5 collective-permute-start.11
  131.7 8.7 %convolution_convert_fusion = bf16[3584,2048]{1,0:T(8,128)(2,1)} fusion(bf16[192,3584]{1,0:T(8,128)(2,1)S(1)} %pad_maximum_fusion, bf16[96,2048]{1,0:T(8,128)(2,1)} %copy-done.16, bf16[96,2048]{1,0:T(8,128)(2,1)S(1)} %copy-done.15), kind=kOutput, calls=%fused_computation | convolution fusion | flops 2827485184 | bytes 16842752 | tf_op jit(solution)/shard_map/dot_general | solution.py:20
  140.4 1.1 constant_dynamic-update-slice_fusion.1
  141.6 0.1 convert_add_fusion.5
  141.7 0.1 collective-permute-start.13
  141.8 0.0 copy-start.9
  141.8 1.1 copy-done.9
  142.9 8.1 %fusion.10 = f32[192,2048]{1,0:T(8,128)S(1)} fusion(bf16[192,3584]{1,0:T(8,128)(2,1)S(1)} %constant_dynamic-update-slice_fusion.right_ref, bf16[2048,3584]{1,0:T(8,128)(2,1)} %param.6), kind=kOutput, calls=%fused_computation.47 | convolution fusion | flops 2818572288 | bytes 17629184 | tf_op jit(solution)/shard_map/dot_general | solution.py:14
  151.0 1.2 pad_maximum_fusion.1.right_ref
  152.2 0.6 collective-permute-done.13
  152.9 1.8 collective-permute-start.14
  154.7 8.1 %fusion.11 = f32[192,2048]{1,0:T(8,128)S(1)} fusion(bf16[192,3584]{1,0:T(8,128)(2,1)S(1)} %pad_maximum_fusion.1.right_ref, bf16[2048,3584]{1,0:T(8,128)(2,1)} %param.7), kind=kOutput, calls=%fused_computation.48 | convolution fusion | flops 2818572288 | bytes 17629184 | tf_op jit(solution)/shard_map/dot_general | solution.py:14
  162.9 0.2 add.131
  163.1 0.1 dynamic-slice_convert_fusion
  163.1 1.2 collective-permute-start.15
  164.4 12.8 %shard_map.93 = bf16[2048,3584]{1,0:T(8,128)(2,1)} custom-call(bf16[2048,192]{1,0:T(8,128)(2,1)} %bitcast.13, bf16[192,3584]{1,0:T(8,128)(2,1)} %copy-done.9), custom_call_target="tpu_custom_call" | custom-call | flops 2818572288 | bytes 16842752 | tf_op jit(solution)/shard_map/pallas_call | solution.py:47
  177.2 0.1 convert_add_fusion.4
  177.3 0.7 collective-permute-start.16
  178.0 12.8 %shard_map.94 = bf16[2048,3584]{1,0:T(8,128)(2,1)} custom-call(bf16[2048,192]{1,0:T(8,128)(2,1)} %bitcast.14, bf16[192,3584]{1,0:T(8,128)(2,1)} %copy-done.7), custom_call_target="tpu_custom_call" | custom-call | flops 2818572288 | bytes 16842752 | tf_op jit(solution)/shard_map/pallas_call | solution.py:47
  190.9 1.8 collective-permute-start.17
  192.7 0.7 add_convert_fusion.1
  193.3 2.2 %collective-permute-done.17 = bf16[24,2048]{1,0:T(8,128)(2,1)S(1)} collective-permute-done((bf16[24,2048]{1,0:T(8,128)(2,1)S(1)}, bf16[24,2048]{1,0:T(8,128)(2,1)S(1)}, u32[]{:S(2)}, u32[]{:S(2)}) %collective-permute-start.17) | collective-permute-done | bytes 98336 | tf_op jit(solution)/shard_map/ppermute | solution.py:200
  195.6 0.7 add_convert_fusion
  (57 shorter events, 0.4 us)
Async XLA Ops:
  20.8 10.2 %copy-start.8 = (bf16[8,24,2048]{2,1,0:T(8,128)(2,1)S(1)}, bf16[8,24,2048]{2,1,0:T(8,128)(2,1)}, u32[]{:S(2)}) copy-start(bf16[8,24,2048]{2,1,0:T(8,128)(2,1)} %shard_map.92) | copy-start | bytes 2359300
  20.8 10.2 %copy-start.21 = (bf16[2048,3584]{1,0:T(8,128)(2,1)S(1)}, bf16[2048,3584]{1,0:T(8,128)(2,1)}, u32[]{:S(2)}) copy-start(bf16[2048,3584]{1,0:T(8,128)(2,1)} %param.7) | copy-start | bytes 44040196
  20.9 10.2 %collective-permute-start = (bf16[24,2048]{1,0:T(8,128)(2,1)}, bf16[24,2048]{1,0:T(8,128)(2,1)S(1)}, u32[]{:S(2)}, u32[]{:S(2)}) collective-permute-start(bf16[24,2048]{1,0:T(8,128)(2,1)} %param.9), channel_id=1, source_target_pairs={{0,8},{4,12},{8,0},{12,4},{16,24},{20,28},{24,16},{28,20},{1,9},{5... | collective-permute-start | bytes 294920 | tf_op jit(solution)/shard_map/ppermute | solution.py:200
  34.1 1.5 copy-start
  34.1 1.5 copy-start.20
  35.7 3.1 %collective-permute-start.2 = (f32[96,3584]{1,0:T(8,128)S(1)}, f32[96,3584]{1,0:T(8,128)S(1)}, u32[]{:S(2)}, u32[]{:S(2)}) collective-permute-start(f32[96,3584]{1,0:T(8,128)S(1)} %slice.26), channel_id=1, source_target_pairs={{0,1},{1,0},{2,3},{3,2},{4,5},{5,4},{6,7},{7,6},{8,9},{9,8},{10,11... | collective-permute-start | bytes 4128776 | tf_op jit(solution)/shard_map/ppermute | solution.py:210
  35.7 12.7 %collective-permute-start.1 = (bf16[48,2048]{1,0:T(8,128)(2,1)S(1)}, bf16[48,2048]{1,0:T(8,128)(2,1)S(1)}, u32[]{:S(2)}, u32[]{:S(2)}) collective-permute-start(bf16[48,2048]{1,0:T(8,128)(2,1)S(1)} %pad_maximum_fusion.6), channel_id=1, source_target_pairs={{0,16},{4,20},{8,24},{12,28},{16,0},{20,4},{24,8},{28,12},{1,17},{... | collective-permute-start | bytes 589832 | tf_op jit(solution)/shard_map/ppermute | solution.py:200
  48.6 11.0 %collective-permute-start.3 = (bf16[96,2048]{1,0:T(8,128)(2,1)S(1)}, bf16[96,2048]{1,0:T(8,128)(2,1)S(1)}, u32[]{:S(2)}, u32[]{:S(2)}) collective-permute-start(bf16[96,2048]{1,0:T(8,128)(2,1)S(1)} %pad_maximum_fusion.5), channel_id=1, source_target_pairs={{0,4},{4,0},{8,12},{12,8},{16,20},{20,16},{24,28},{28,24},{1,5},{5... | collective-permute-start | bytes 1179656 | tf_op jit(solution)/shard_map/ppermute | solution.py:200
  52.2 20.3 %collective-permute-start.5 = (bf16[96,3584]{1,0:T(8,128)(2,1)}, bf16[96,3584]{1,0:T(8,128)(2,1)S(1)}, u32[]{:S(2)}, u32[]{:S(2)}) collective-permute-start(bf16[96,3584]{1,0:T(8,128)(2,1)} %slice.56), channel_id=1, source_target_pairs={{0,1},{1,0},{2,3},{3,2},{4,5},{5,4},{6,7},{7,6},{8,9},{9,8},{10,11... | collective-permute-start | bytes 2064392 | tf_op jit(solution)/shard_map/ppermute | solution.py:210
  59.7 8.5 %copy-start.14 = (bf16[96,2048]{1,0:T(8,128)(2,1)}, bf16[96,2048]{1,0:T(8,128)(2,1)S(1)}, u32[]{:S(2)}) copy-start(bf16[96,2048]{1,0:T(8,128)(2,1)S(1)} %get-tuple-element.71) | copy-start | bytes 1179652
  59.7 8.5 %copy-start.16 = (bf16[96,2048]{1,0:T(8,128)(2,1)}, bf16[96,2048]{1,0:T(8,128)(2,1)S(1)}, u32[]{:S(2)}) copy-start(bf16[96,2048]{1,0:T(8,128)(2,1)S(1)} %get-tuple-element.72) | copy-start | bytes 1179652
  68.2 2.0 %copy-start.5 = (f32[192,3584]{1,0:T(8,128)}, f32[192,3584]{1,0:T(8,128)S(1)}, u32[]{:S(2)}) copy-start(f32[192,3584]{1,0:T(8,128)S(1)} %fusion.1) | copy-start | bytes 8257540
  70.2 6.0 %collective-permute-start.4 = (f32[96,3584]{1,0:T(8,128)}, f32[96,3584]{1,0:T(8,128)S(1)}, u32[]{:S(2)}, u32[]{:S(2)}) collective-permute-start(f32[96,3584]{1,0:T(8,128)} %slice.28), channel_id=1, source_target_pairs={{0,1},{1,0},{2,3},{3,2},{4,5},{5,4},{6,7},{7,6},{8,9},{9,8},{10,11... | collective-permute-start | bytes 4128776 | tf_op jit(solution)/shard_map/ppermute | solution.py:210
  72.5 3.2 %copy-start.19 = (bf16[96,3584]{1,0:T(8,128)(2,1)S(1)}, bf16[96,3584]{1,0:T(8,128)(2,1)}, u32[]{:S(2)}) copy-start(bf16[96,3584]{1,0:T(8,128)(2,1)} %fusion.5) | copy-start | bytes 2064388
  72.5 34.3 %copy-start.3 = (f32[192,3584]{1,0:T(8,128)S(1)}, f32[192,3584]{1,0:T(8,128)}, u32[]{:S(2)}) copy-start(f32[192,3584]{1,0:T(8,128)} %fusion.8) | copy-start | bytes 8257540
  74.1 32.7 %copy-start.1 = (f32[192,3584]{1,0:T(8,128)S(1)}, f32[192,3584]{1,0:T(8,128)}, u32[]{:S(2)}) copy-start(f32[192,3584]{1,0:T(8,128)} %copy-done) | copy-start | bytes 8257540
  74.1 18.4 %collective-permute-start.6 = (bf16[96,3584]{1,0:T(8,128)(2,1)S(1)}, bf16[96,3584]{1,0:T(8,128)(2,1)S(1)}, u32[]{:S(2)}, u32[]{:S(2)}) collective-permute-start(bf16[96,3584]{1,0:T(8,128)(2,1)S(1)} %fusion.2), channel_id=1, source_target_pairs={{0,2},{1,3},{2,0},{3,1},{4,6},{5,7},{6,4},{7,5},{8,10},{9,11},{10,... | collective-permute-start | bytes 2064392 | tf_op jit(solution)/shard_map/ppermute | solution.py:206
  75.7 31.1 %collective-permute-start.7 = (bf16[96,3584]{1,0:T(8,128)(2,1)S(1)}, bf16[96,3584]{1,0:T(8,128)(2,1)S(1)}, u32[]{:S(2)}, u32[]{:S(2)}) collective-permute-start(bf16[96,3584]{1,0:T(8,128)(2,1)S(1)} %copy-done.19), channel_id=1, source_target_pairs={{0,2},{1,3},{2,0},{3,1},{4,6},{5,7},{6,4},{7,5},{8,10},{9,11},{10,... | collective-permute-start | bytes 2064392 | tf_op jit(solution)/shard_map/ppermute | solution.py:206
  92.5 15.8 %copy-start.10 = (bf16[96,3584]{1,0:T(8,128)(2,1)}, bf16[96,3584]{1,0:T(8,128)(2,1)S(1)}, u32[]{:S(2)}) copy-start(bf16[96,3584]{1,0:T(8,128)(2,1)S(1)} %collective-permute-done.6) | copy-start | bytes 2064388
  106.7 1.6 copy-start.12
  108.3 2.5 %collective-permute-start.9 = (bf16[96,3584]{1,0:T(8,128)(2,1)}, bf16[96,3584]{1,0:T(8,128)(2,1)}, u32[]{:S(2)}, u32[]{:S(2)}) collective-permute-start(bf16[96,3584]{1,0:T(8,128)(2,1)} %multiply_convert_fusion.2), channel_id=1, source_target_pairs={{0,1},{1,0},{2,3},{3,2},{4,5},{5,4},{6,7},{7,6},{8,9},{9,8},{10,11... | collective-permute-start | bytes 2064392 | tf_op jit(solution)/shard_map/ppermute | solution.py:210
  108.4 18.0 %collective-permute-start.8 = (bf16[96,3584]{1,0:T(8,128)(2,1)}, bf16[96,3584]{1,0:T(8,128)(2,1)S(1)}, u32[]{:S(2)}, u32[]{:S(2)}) collective-permute-start(bf16[96,3584]{1,0:T(8,128)(2,1)} %fusion.6), channel_id=1, source_target_pairs={{0,2},{1,3},{2,0},{3,1},{4,6},{5,7},{6,4},{7,5},{8,10},{9,11},{10,... | collective-permute-start | bytes 2064392 | tf_op jit(solution)/shard_map/ppermute | solution.py:206
  110.8 17.0 %copy-start.4 = (f32[192,3584]{1,0:T(8,128)S(1)}, f32[192,3584]{1,0:T(8,128)}, u32[]{:S(2)}) copy-start(f32[192,3584]{1,0:T(8,128)} %fusion.8) | copy-start | bytes 8257540
  110.8 17.0 %copy-start.6 = (f32[192,3584]{1,0:T(8,128)S(1)}, f32[192,3584]{1,0:T(8,128)}, u32[]{:S(2)}) copy-start(f32[192,3584]{1,0:T(8,128)} %copy-done.5) | copy-start | bytes 8257540
  110.8 17.0 %copy-start.11 = (bf16[96,3584]{1,0:T(8,128)(2,1)S(1)}, bf16[96,3584]{1,0:T(8,128)(2,1)}, u32[]{:S(2)}) copy-start(bf16[96,3584]{1,0:T(8,128)(2,1)} %copy-done.10) | copy-start | bytes 2064388
  110.8 17.0 %copy-start.13 = (bf16[96,3584]{1,0:T(8,128)(2,1)S(1)}, bf16[96,3584]{1,0:T(8,128)(2,1)}, u32[]{:S(2)}) copy-start(bf16[96,3584]{1,0:T(8,128)(2,1)} %copy-done.12) | copy-start | bytes 2064388
  118.2 11.8 %copy-start.17 = (f32[192,2048]{1,0:T(8,128)}, f32[192,2048]{1,0:T(8,128)S(1)}, u32[]{:S(2)}) copy-start(f32[192,2048]{1,0:T(8,128)S(1)} %fusion.7) | copy-start | bytes 4718596
  118.2 9.6 %copy-start.2 = (f32[192,3584]{1,0:T(8,128)S(1)}, f32[192,3584]{1,0:T(8,128)}, u32[]{:S(2)}) copy-start(f32[192,3584]{1,0:T(8,128)} %copy-done) | copy-start | bytes 8257540
  127.8 3.8 %copy-start.15 = (bf16[96,2048]{1,0:T(8,128)(2,1)S(1)}, bf16[96,2048]{1,0:T(8,128)(2,1)}, u32[]{:S(2)}) copy-start(bf16[96,2048]{1,0:T(8,128)(2,1)} %copy-done.14) | copy-start | bytes 1179652
  130.0 11.5 %collective-permute-start.12 = (bf16[96,2048]{1,0:T(8,128)(2,1)S(1)}, bf16[96,2048]{1,0:T(8,128)(2,1)S(1)}, u32[]{:S(2)}, u32[]{:S(2)}) collective-permute-start(bf16[96,2048]{1,0:T(8,128)(2,1)S(1)} %dynamic-slice_convert_fusion.1), channel_id=1, source_target_pairs={{0,4},{4,0},{8,12},{12,8},{16,20},{20,16},{24,28},{28,24},{1,5},{5... | collective-permute-start | bytes 1179656 | tf_op jit(solution)/shard_map/ppermute | solution.py:200
  131.2 10.4 %collective-permute-start.10 = (bf16[96,3584]{1,0:T(8,128)(2,1)}, bf16[96,3584]{1,0:T(8,128)(2,1)S(1)}, u32[]{:S(2)}, u32[]{:S(2)}) collective-permute-start(bf16[96,3584]{1,0:T(8,128)(2,1)} %get-tuple-element.49), channel_id=1, source_target_pairs={{0,1},{1,0},{2,3},{3,2},{4,5},{5,4},{6,7},{7,6},{8,9},{9,8},{10,11... | collective-permute-start | bytes 2064392 | tf_op jit(solution)/shard_map/ppermute | solution.py:210
  131.2 10.4 %collective-permute-start.11 = (bf16[96,3584]{1,0:T(8,128)(2,1)}, bf16[96,3584]{1,0:T(8,128)(2,1)S(1)}, u32[]{:S(2)}, u32[]{:S(2)}) collective-permute-start(bf16[96,3584]{1,0:T(8,128)(2,1)} %get-tuple-element.50), channel_id=1, source_target_pairs={{0,1},{1,0},{2,3},{3,2},{4,5},{5,4},{6,7},{7,6},{8,9},{9,8},{10,11... | collective-permute-start | bytes 2064392 | tf_op jit(solution)/shard_map/ppermute | solution.py:210
  131.7 9.9 %copy-start.18 = (f32[192,2048]{1,0:T(8,128)S(1)}, f32[192,2048]{1,0:T(8,128)}, u32[]{:S(2)}) copy-start(f32[192,2048]{1,0:T(8,128)} %copy-done.17) | copy-start | bytes 4718596
  141.7 11.2 %collective-permute-start.13 = (bf16[48,2048]{1,0:T(8,128)(2,1)S(1)}, bf16[48,2048]{1,0:T(8,128)(2,1)S(1)}, u32[]{:S(2)}, u32[]{:S(2)}) collective-permute-start(bf16[48,2048]{1,0:T(8,128)(2,1)S(1)} %dynamic-slice_convert_fusion.3), channel_id=1, source_target_pairs={{0,16},{4,20},{8,24},{12,28},{16,0},{20,4},{24,8},{28,12},{1,17},{... | collective-permute-start | bytes 589832 | tf_op jit(solution)/shard_map/ppermute | solution.py:200
  141.8 1.1 copy-start.9
  152.2 10.6 %copy-start.7 = (bf16[192,3584]{1,0:T(8,128)(2,1)}, bf16[192,3584]{1,0:T(8,128)(2,1)S(1)}, u32[]{:S(2)}) copy-start(bf16[192,3584]{1,0:T(8,128)(2,1)S(1)} %pad_maximum_fusion.1.right_ref) | copy-start | bytes 4128772
  152.9 10.2 %collective-permute-start.14 = (bf16[24,2048]{1,0:T(8,128)(2,1)S(1)}, bf16[24,2048]{1,0:T(8,128)(2,1)S(1)}, u32[]{:S(2)}, u32[]{:S(2)}) collective-permute-start(bf16[24,2048]{1,0:T(8,128)(2,1)S(1)} %dynamic-slice_convert_fusion.5), channel_id=1, source_target_pairs={{0,8},{4,12},{8,0},{12,4},{16,24},{20,28},{24,16},{28,20},{1,9},{5... | collective-permute-start | bytes 294920 | tf_op jit(solution)/shard_map/ppermute | solution.py:200
  163.1 14.0 %collective-permute-start.15 = (bf16[96,2048]{1,0:T(8,128)(2,1)S(1)}, bf16[96,2048]{1,0:T(8,128)(2,1)S(1)}, u32[]{:S(2)}, u32[]{:S(2)}) collective-permute-start(bf16[96,2048]{1,0:T(8,128)(2,1)S(1)} %dynamic-slice_convert_fusion), channel_id=1, source_target_pairs={{0,4},{4,0},{8,12},{12,8},{16,20},{20,16},{24,28},{28,24},{1,5},{5... | collective-permute-start | bytes 1179656 | tf_op jit(solution)/shard_map/ppermute | solution.py:200
  177.3 13.6 %collective-permute-start.16 = (bf16[48,2048]{1,0:T(8,128)(2,1)S(1)}, bf16[48,2048]{1,0:T(8,128)(2,1)S(1)}, u32[]{:S(2)}, u32[]{:S(2)}) collective-permute-start(bf16[48,2048]{1,0:T(8,128)(2,1)S(1)} %dynamic-slice_convert_fusion.2), channel_id=1, source_target_pairs={{0,16},{4,20},{8,24},{12,28},{16,0},{20,4},{24,8},{28,12},{1,17},{... | collective-permute-start | bytes 589832 | tf_op jit(solution)/shard_map/ppermute | solution.py:200
  190.9 4.7 %collective-permute-start.17 = (bf16[24,2048]{1,0:T(8,128)(2,1)S(1)}, bf16[24,2048]{1,0:T(8,128)(2,1)S(1)}, u32[]{:S(2)}, u32[]{:S(2)}) collective-permute-start(bf16[24,2048]{1,0:T(8,128)(2,1)S(1)} %dynamic-slice_convert_fusion.4), channel_id=1, source_target_pairs={{0,8},{4,12},{8,0},{12,4},{16,24},{20,28},{24,16},{28,20},{1,9},{5... | collective-permute-start | bytes 294920 | tf_op jit(solution)/shard_map/ppermute | solution.py:200
where the time goes:
time: 198 us; the launch traced here: 196 us
  waiting for transfers between devices  54.9 us (28%)
  matrix products  54 us (27%)
  Pallas kernels  45.8 us (23%)
  starting transfers between devices  15.4 us (8%)
  other arithmetic  14.5 us (7%)
  local copies, waits for them, and re-layouts  10.5 us (5%)
    ppermute x3, waiting for transfers between devices, x_move(): return lax.ppermute(value, 'col', pairs)  36.4 us
    pallas_call x2, Pallas kernels, weight_grad(): pl.pallas_call(weight_grad_kernel, grid=(cols // tile,), in_specs=[pl.Blo...  25.6 us
    dot_general x3, matrix products, contract_last(): lax.dot_general(left, right, (((1,), (1,)), ((), ())), preferred_element_...  24.8 us
    dot_general x3, matrix products, contract_mid(): return jnp.dot(left, right, preferred_element_type=jnp.float32)  20.5 us
    pallas_call x1, Pallas kernels, gather_rows(): pl.pallas_call(functools.partial(gather_kernel, n_z, n_y, cores), out_sha...  20.2 us
    ppermute x9, waiting for transfers between devices, row_swap(): return lax.ppermute(value, 'row', [(r, r ^ bit) for r in range(n_row)])  17.5 us
    ppermute x9, starting transfers between devices, row_swap(): return lax.ppermute(value, 'row', [(r, r ^ bit) for r in range(n_row)])  11.2 us
    dot_general x1, matrix products, contract_first(): lax.dot_general(left, right, (((0,), (0,)), ((), ())), preferred_element_...  8.69 us
  transfers between devices with their start and end apart: 18, of which 9 were waited for; matrix products, arithmetic and copies ran while one was open for 34% of the time, Pallas kernels for 13%

commit v1 on v0

--- a/solution.py
+++ b/solution.py
@@ -43,7 +43,7 @@
 def weight_grad(left_t, right):
     rows, tokens = left_t.shape
     cols = right.shape[1]
-    tile = tile_of(cols, 256)
+    tile = tile_of(cols, 512)
     return pl.pallas_call(
         weight_grad_kernel,
         grid=(cols // tile,),
@@ -280,14 +280,16 @@
         arrived, up_sent = tie((arrived, up_mine.astype(BF16)))
         up_moved = send_x(up_sent)
         grad_all = both(arrived)
+        inputs_t = inputs_all.T
         while bit < n_row // 2:
             bit *= 2
             arrived, both = gather_step(grad_all, bit)
+            arrived, inputs_t = tie((arrived, inputs_t))
             grad_all = both(arrived)
         d_part = contract_last(grad_all, down_weight)
         d_mine = sum_core(d_part, jnp.float32)
         d_sent, gate_moved, up_moved, inputs_t = tie(
-            (d_mine.astype(BF16), gate_moved, up_moved, inputs_all.T)
+            (d_mine.astype(BF16), gate_moved, up_moved, inputs_t)
         )
         d_moved = send_x(d_sent)
         gate_pre, up_pre = add_all(gate_mine, gate_moved), add_all(up_mine, up_moved)

time: 198 us -> 185 us (0.934)
  Pallas kernels: 45.8 us -> 39.6 us
  other arithmetic: 14.5 us -> 10.6 us
  local copies, waits for them, and re-layouts: 10.5 us -> 8.34 us
    pallas_call x2, Pallas kernels: 25.6 us -> 19.4 us  [weight_grad(): pl.pallas_call(weight_grad_kernel, grid=(cols // tile,), in_specs=[pl.Blo...]
    slice x3, local copies, waits for them, and re-layouts: 3.69 us -> 1.59 us  [sum_core(): part[rows:].astype(dtype)]
  transfers between devices with their start and end apart: 18 -> 18, of which waited for: 9 -> 9; matrix products, arithmetic and copies ran while one was open for 34% -> 32% of each run, Pallas kernels for 13% -> 11%
where the time goes in v1:
time: 185 us; the launch traced here: 184 us
  waiting for transfers between devices  56.4 us (30%)
  matrix products  54 us (29%)
  Pallas kernels  39.6 us (21%)
  starting transfers between devices  14.4 us (8%)
  other arithmetic  10.6 us (6%)
  local copies, waits for them, and re-layouts  8.34 us (5%)
    ppermute x3, waiting for transfers between devices, x_move(): return lax.ppermute(value, 'col', pairs)  36.2 us
    dot_general x3, matrix products, contract_last(): lax.dot_general(left, right, (((1,), (1,)), ((), ())), preferred_element_...  24.8 us
    dot_general x3, matrix products, contract_mid(): return jnp.dot(left, right, preferred_element_type=jnp.float32)  20.5 us
    pallas_call x1, Pallas kernels, gather_rows(): pl.pallas_call(functools.partial(gather_kernel, n_z, n_y, cores), out_sha...  20.2 us
    pallas_call x2, Pallas kernels, weight_grad(): pl.pallas_call(weight_grad_kernel, grid=(cols // tile,), in_specs=[pl.Blo...  19.4 us
    ppermute x9, waiting for transfers between devices, row_swap(): return lax.ppermute(value, 'row', [(r, r ^ bit) for r in range(n_row)])  19.3 us
    ppermute x9, starting transfers between devices, row_swap(): return lax.ppermute(value, 'row', [(r, r ^ bit) for r in range(n_row)])  10.1 us
    dot_general x1, matrix products, contract_first(): lax.dot_general(left, right, (((0,), (0,)), ((), ())), preferred_element_...  8.7 us
  transfers between devices with their start and end apart: 18, of which 9 were waited for; matrix products, arithmetic and copies ran while one was open for 32% of the time, Pallas kernels for 11%

profile of v1, /device:TPU:0, one launch (start us, length us, event | category | flops | bytes accessed | tf_op | source)
XLA Modules:
  0.0 184.5 jit_solution(6504463284638050515)
XLA Ops:
  0.6 20.2 %shard_map.92 = bf16[8,24,2048]{2,1,0:T(8,128)(2,1)} custom-call(bf16[24,2048]{1,0:T(8,128)(2,1)} %refs_0_.1), custom_call_target="tpu_custom_call" | custom-call | bytes 3145728 | tf_op jit(solution)/shard_map/pallas_call | solution.py:178
  20.8 0.0 copy-start.21
  20.9 0.1 collective-permute-start
  20.9 10.1 %fusion.8 = f32[192,3584]{1,0:T(8,128)} fusion(bf16[192,2048]{1,0:T(8,128)(2,1)} %bitcast.15, bf16[2048,3584]{1,0:T(8,128)(2,1)} %param.6), kind=kOutput, calls=%fused_computation.45 | convolution fusion | flops 2818572288 | bytes 18219008 | tf_op jit(solution)/shard_map/dot_general | solution.py:26
  31.1 0.0 copy-start.20
  31.1 3.1 %fusion.9 = f32[192,3584]{1,0:T(8,128)S(1)} fusion(bf16[192,2048]{1,0:T(8,128)(2,1)S(1)} %bitcast.16, bf16[2048,3584]{1,0:T(8,128)(2,1)S(1)} %copy-done.21), kind=kOutput, calls=%fused_computation.46 | convolution fusion | flops 2818572288 | bytes 18219008 | tf_op jit(solution)/shard_map/dot_general | solution.py:26
  34.2 0.0 copy-start
  34.2 0.1 slice.26
  34.3 1.4 copy-done
  35.7 1.0 broadcast_select_fusion.5
  36.7 2.9 %collective-permute-start.1 = (bf16[48,2048]{1,0:T(8,128)(2,1)S(1)}, bf16[48,2048]{1,0:T(8,128)(2,1)S(1)}, u32[]{:S(2)}, u32[]{:S(2)}) collective-permute-start(bf16[48,2048]{1,0:T(8,128)(2,1)S(1)} %pad_maximum_fusion.6), channel_id=1, source_target_pairs={{0,16},{4,20},{8,24},{12,28},{16,0},{20,4},{24,8},{28,12},{1,17},{... | collective-permute-start | bytes 589832 | tf_op jit(solution)/shard_map/ppermute | solution.py:200
  39.6 2.3 %fusion.5 = bf16[96,3584]{1,0:T(8,128)(2,1)} fusion(f32[96,3584]{1,0:T(8,128)S(1)} %collective-permute-done.2, f32[192,3584]{1,0:T(8,128)} %copy-done), kind=kLoop, calls=%fused_computation.42 | loop fusion | flops 688128 | bytes 3440640 | tf_op jit(solution)/shard_map/convert_element_type | solution.py:280
  41.9 7.5 %collective-permute-done.1 = bf16[48,2048]{1,0:T(8,128)(2,1)S(1)} collective-permute-done((bf16[48,2048]{1,0:T(8,128)(2,1)S(1)}, bf16[48,2048]{1,0:T(8,128)(2,1)S(1)}, u32[]{:S(2)}, u32[]{:S(2)}) %collective-permute-start.1) | collective-permute-done | bytes 196640 | tf_op jit(solution)/shard_map/ppermute | solution.py:200
  49.4 0.1 broadcast_select_fusion.3
  49.5 1.4 collective-permute-start.3
  50.9 1.3 copy.11
  52.2 1.4 slice.56
  53.6 0.1 collective-permute-start.5
  53.7 6.8 %collective-permute-done.3 = bf16[96,2048]{1,0:T(8,128)(2,1)S(1)} collective-permute-done((bf16[96,2048]{1,0:T(8,128)(2,1)S(1)}, bf16[96,2048]{1,0:T(8,128)(2,1)S(1)}, u32[]{:S(2)}, u32[]{:S(2)}) %collective-permute-start.3) | collective-permute-done | bytes 393248 | tf_op jit(solution)/shard_map/ppermute | solution.py:200
  60.5 0.1 broadcast_select_fusion.1
  60.6 8.5 %fusion.1 = f32[192,3584]{1,0:T(8,128)S(1)} fusion(bf16[3584,2048]{1,0:T(8,128)(2,1)} %param.8, bf16[96,2048]{1,0:T(8,128)(2,1)S(1)} %get-tuple-element.76, bf16[96,2048]{1,0:T(8,128)(2,1)S(1)} %get-tuple-element.75), kind=kOutput, calls=%fused_computation.20 | convolution fusion | flops 2820145152 | bytes 18219008 | tf_op jit(solution)/shard_map/dot_general | solution.py:14
  69.2 0.0 copy-start.5
  69.2 0.0 copy-start.3
  69.2 0.1 slice.28
  69.3 0.1 collective-permute-start.4
  69.4 2.6 %copy-done.3 = f32[192,3584]{1,0:T(8,128)S(1)} copy-done((f32[192,3584]{1,0:T(8,128)S(1)}, f32[192,3584]{1,0:T(8,128)}, u32[]{:S(2)}) %copy-start.3) | copy-done | bytes 2752536
  72.0 0.1 fusion.2
  72.1 0.0 copy-start.1
  72.1 1.6 collective-permute-start.6
  73.7 0.5 collective-permute-start.7
  74.2 1.0 fusion.6
  75.3 15.2 %collective-permute-done.6 = bf16[96,3584]{1,0:T(8,128)(2,1)S(1)} collective-permute-done((bf16[96,3584]{1,0:T(8,128)(2,1)S(1)}, bf16[96,3584]{1,0:T(8,128)(2,1)S(1)}, u32[]{:S(2)}, u32[]{:S(2)}) %collective-permute-start.6) | collective-permute-done | bytes 688160 | tf_op jit(solution)/shard_map/ppermute | solution.py:206
  90.5 12.8 %collective-permute-done.7 = bf16[96,3584]{1,0:T(8,128)(2,1)S(1)} collective-permute-done((bf16[96,3584]{1,0:T(8,128)(2,1)S(1)}, bf16[96,3584]{1,0:T(8,128)(2,1)S(1)}, u32[]{:S(2)}, u32[]{:S(2)}) %collective-permute-start.7) | collective-permute-done | bytes 688160 | tf_op jit(solution)/shard_map/ppermute | solution.py:206
  103.3 1.6 multiply_convert_fusion.2
  104.9 1.6 collective-permute-start.8
  106.5 0.9 collective-permute-done.9
  107.4 7.3 %fusion.7 = f32[192,2048]{1,0:T(8,128)S(1)} fusion(bf16[3584,2048]{1,0:T(8,128)(2,1)} %param.8, bf16[96,3584]{1,0:T(8,128)(2,1)} %collective-permute-done.9, bf16[96,3584]{1,0:T(8,128)(2,1)} %multiply_convert_fusion.2), kind=kOutput, calls=%fused_computation.44 | convolution fusion | flops 2821324800 | bytes 17629184 | tf_op jit(solution)/shard_map/dot_general | solution.py:26
  114.8 8.2 %collective-permute-done.8 = bf16[96,3584]{1,0:T(8,128)(2,1)S(1)} collective-permute-done((bf16[96,3584]{1,0:T(8,128)(2,1)}, bf16[96,3584]{1,0:T(8,128)(2,1)S(1)}, u32[]{:S(2)}, u32[]{:S(2)}) %collective-permute-start.8) | collective-permute-done | bytes 688160 | tf_op jit(solution)/shard_map/ppermute | solution.py:206
  123.0 1.4 pad_maximum_fusion
  124.4 1.1 multiply_convert_fusion
  125.5 0.1 dynamic-slice_convert_fusion.1
  125.6 0.9 collective-permute-start.12
  126.5 0.5 collective-permute-start.11
  127.0 8.7 %convolution_convert_fusion = bf16[3584,2048]{1,0:T(8,128)(2,1)} fusion(bf16[192,3584]{1,0:T(8,128)(2,1)S(1)} %pad_maximum_fusion, bf16[96,2048]{1,0:T(8,128)(2,1)} %copy-done.16, bf16[96,2048]{1,0:T(8,128)(2,1)S(1)} %copy-done.15), kind=kOutput, calls=%fused_computation | convolution fusion | flops 2827485184 | bytes 16842752 | tf_op jit(solution)/shard_map/dot_general | solution.py:20
  135.8 0.4 collective-permute-done.12
  136.2 0.1 convert_add_fusion.5
  136.3 0.1 collective-permute-start.13
  136.5 1.1 copy-done.9
  137.6 8.1 %fusion.10 = f32[192,2048]{1,0:T(8,128)S(1)} fusion(bf16[192,3584]{1,0:T(8,128)(2,1)S(1)} %constant_dynamic-update-slice_fusion.right_ref, bf16[2048,3584]{1,0:T(8,128)(2,1)} %param.6), kind=kOutput, calls=%fused_computation.47 | convolution fusion | flops 2818572288 | bytes 17629184 | tf_op jit(solution)/shard_map/dot_general | solution.py:14
  145.7 0.1 pad_maximum_fusion.1.right_ref
  145.8 1.3 collective-permute-done.13
  147.2 1.1 collective-permute-start.14
  148.3 8.1 %fusion.11 = f32[192,2048]{1,0:T(8,128)S(1)} fusion(bf16[192,3584]{1,0:T(8,128)(2,1)S(1)} %pad_maximum_fusion.1.right_ref, bf16[2048,3584]{1,0:T(8,128)(2,1)} %param.7), kind=kOutput, calls=%fused_computation.48 | convolution fusion | flops 2818572288 | bytes 17629184 | tf_op jit(solution)/shard_map/dot_general | solution.py:14
  156.5 0.2 add.131
  156.7 0.1 dynamic-slice_convert_fusion
  156.7 1.0 collective-permute-start.15
  157.7 9.7 %shard_map.93 = bf16[2048,3584]{1,0:T(8,128)(2,1)} custom-call(bf16[2048,192]{1,0:T(8,128)(2,1)} %bitcast.13, bf16[192,3584]{1,0:T(8,128)(2,1)} %copy-done.9), custom_call_target="tpu_custom_call" | custom-call | flops 2818572288 | bytes 16842752 | tf_op jit(solution)/shard_map/pallas_call | solution.py:47
  167.4 0.1 convert_add_fusion.4
  167.6 1.8 collective-permute-start.16
  169.4 9.7 %shard_map.94 = bf16[2048,3584]{1,0:T(8,128)(2,1)} custom-call(bf16[2048,192]{1,0:T(8,128)(2,1)} %bitcast.14, bf16[192,3584]{1,0:T(8,128)(2,1)} %copy-done.7), custom_call_target="tpu_custom_call" | custom-call | flops 2818572288 | bytes 16842752 | tf_op jit(solution)/shard_map/pallas_call | solution.py:47
  179.1 0.8 collective-permute-start.17
  180.0 0.7 add_convert_fusion.1
  180.6 3.2 %collective-permute-done.17 = bf16[24,2048]{1,0:T(8,128)(2,1)S(1)} collective-permute-done((bf16[24,2048]{1,0:T(8,128)(2,1)S(1)}, bf16[24,2048]{1,0:T(8,128)(2,1)S(1)}, u32[]{:S(2)}, u32[]{:S(2)}) %collective-permute-start.17) | collective-permute-done | bytes 98336 | tf_op jit(solution)/shard_map/ppermute | solution.py:200
  183.8 0.7 add_convert_fusion
  (57 shorter events, 0.4 us)
Async XLA Ops:
  20.8 10.2 %copy-start.8 = (bf16[8,24,2048]{2,1,0:T(8,128)(2,1)S(1)}, bf16[8,24,2048]{2,1,0:T(8,128)(2,1)}, u32[]{:S(2)}) copy-start(bf16[8,24,2048]{2,1,0:T(8,128)(2,1)} %shard_map.92) | copy-start | bytes 2359300
  20.8 10.2 %copy-start.21 = (bf16[2048,3584]{1,0:T(8,128)(2,1)S(1)}, bf16[2048,3584]{1,0:T(8,128)(2,1)}, u32[]{:S(2)}) copy-start(bf16[2048,3584]{1,0:T(8,128)(2,1)} %param.7) | copy-start | bytes 44040196
  20.9 10.2 %collective-permute-start = (bf16[24,2048]{1,0:T(8,128)(2,1)}, bf16[24,2048]{1,0:T(8,128)(2,1)S(1)}, u32[]{:S(2)}, u32[]{:S(2)}) collective-permute-start(bf16[24,2048]{1,0:T(8,128)(2,1)} %param.9), channel_id=1, source_target_pairs={{0,8},{4,12},{8,0},{12,4},{16,24},{20,28},{24,16},{28,20},{1,9},{5... | collective-permute-start | bytes 294920 | tf_op jit(solution)/shard_map/ppermute | solution.py:200
  31.1 3.1 %copy-start.20 = (bf16[24,2048]{1,0:T(8,128)(2,1)}, bf16[24,2048]{1,0:T(8,128)(2,1)S(1)}, u32[]{:S(2)}) copy-start(bf16[24,2048]{1,0:T(8,128)(2,1)S(1)} %collective-permute-done) | copy-start | bytes 294916
  34.2 1.5 copy-start
  35.7 3.9 %collective-permute-start.2 = (f32[96,3584]{1,0:T(8,128)S(1)}, f32[96,3584]{1,0:T(8,128)S(1)}, u32[]{:S(2)}, u32[]{:S(2)}) collective-permute-start(f32[96,3584]{1,0:T(8,128)S(1)} %slice.26), channel_id=1, source_target_pairs={{0,1},{1,0},{2,3},{3,2},{4,5},{5,4},{6,7},{7,6},{8,9},{9,8},{10,11... | collective-permute-start | bytes 4128776 | tf_op jit(solution)/shard_map/ppermute | solution.py:210
  36.7 12.7 %collective-permute-start.1 = (bf16[48,2048]{1,0:T(8,128)(2,1)S(1)}, bf16[48,2048]{1,0:T(8,128)(2,1)S(1)}, u32[]{:S(2)}, u32[]{:S(2)}) collective-permute-start(bf16[48,2048]{1,0:T(8,128)(2,1)S(1)} %pad_maximum_fusion.6), channel_id=1, source_target_pairs={{0,16},{4,20},{8,24},{12,28},{16,0},{20,4},{24,8},{28,12},{1,17},{... | collective-permute-start | bytes 589832 | tf_op jit(solution)/shard_map/ppermute | solution.py:200
  49.5 11.0 %collective-permute-start.3 = (bf16[96,2048]{1,0:T(8,128)(2,1)S(1)}, bf16[96,2048]{1,0:T(8,128)(2,1)S(1)}, u32[]{:S(2)}, u32[]{:S(2)}) collective-permute-start(bf16[96,2048]{1,0:T(8,128)(2,1)S(1)} %pad_maximum_fusion.5), channel_id=1, source_target_pairs={{0,4},{4,0},{8,12},{12,8},{16,20},{20,16},{24,28},{28,24},{1,5},{5... | collective-permute-start | bytes 1179656 | tf_op jit(solution)/shard_map/ppermute | solution.py:200
  53.6 15.8 %collective-permute-start.5 = (bf16[96,3584]{1,0:T(8,128)(2,1)S(1)}, bf16[96,3584]{1,0:T(8,128)(2,1)S(1)}, u32[]{:S(2)}, u32[]{:S(2)}) collective-permute-start(bf16[96,3584]{1,0:T(8,128)(2,1)S(1)} %slice.56), channel_id=1, source_target_pairs={{0,1},{1,0},{2,3},{3,2},{4,5},{5,4},{6,7},{7,6},{8,9},{9,8},{10,11... | collective-permute-start | bytes 2064392 | tf_op jit(solution)/shard_map/ppermute | solution.py:210
  60.6 8.6 %copy-start.14 = (bf16[96,2048]{1,0:T(8,128)(2,1)}, bf16[96,2048]{1,0:T(8,128)(2,1)S(1)}, u32[]{:S(2)}) copy-start(bf16[96,2048]{1,0:T(8,128)(2,1)S(1)} %get-tuple-element.75) | copy-start | bytes 1179652
  60.6 8.6 %copy-start.16 = (bf16[96,2048]{1,0:T(8,128)(2,1)}, bf16[96,2048]{1,0:T(8,128)(2,1)S(1)}, u32[]{:S(2)}) copy-start(bf16[96,2048]{1,0:T(8,128)(2,1)S(1)} %get-tuple-element.76) | copy-start | bytes 1179652
  69.2 5.0 %copy-start.5 = (f32[192,3584]{1,0:T(8,128)}, f32[192,3584]{1,0:T(8,128)S(1)}, u32[]{:S(2)}) copy-start(f32[192,3584]{1,0:T(8,128)S(1)} %fusion.1) | copy-start | bytes 8257540
  69.2 2.8 %copy-start.3 = (f32[192,3584]{1,0:T(8,128)S(1)}, f32[192,3584]{1,0:T(8,128)}, u32[]{:S(2)}) copy-start(f32[192,3584]{1,0:T(8,128)} %fusion.8) | copy-start | bytes 8257540
  69.3 4.4 %copy-start.19 = (bf16[96,3584]{1,0:T(8,128)(2,1)S(1)}, bf16[96,3584]{1,0:T(8,128)(2,1)}, u32[]{:S(2)}) copy-start(bf16[96,3584]{1,0:T(8,128)(2,1)} %fusion.5) | copy-start | bytes 2064388
  69.3 4.9 %collective-permute-start.4 = (f32[96,3584]{1,0:T(8,128)S(1)}, f32[96,3584]{1,0:T(8,128)S(1)}, u32[]{:S(2)}, u32[]{:S(2)}) collective-permute-start(f32[96,3584]{1,0:T(8,128)S(1)} %slice.28), channel_id=1, source_target_pairs={{0,1},{1,0},{2,3},{3,2},{4,5},{5,4},{6,7},{7,6},{8,9},{9,8},{10,11... | collective-permute-start | bytes 4128776 | tf_op jit(solution)/shard_map/ppermute | solution.py:210
  72.1 31.2 %copy-start.1 = (f32[192,3584]{1,0:T(8,128)S(1)}, f32[192,3584]{1,0:T(8,128)}, u32[]{:S(2)}) copy-start(f32[192,3584]{1,0:T(8,128)} %copy-done) | copy-start | bytes 8257540
  72.1 18.4 %collective-permute-start.6 = (bf16[96,3584]{1,0:T(8,128)(2,1)S(1)}, bf16[96,3584]{1,0:T(8,128)(2,1)S(1)}, u32[]{:S(2)}, u32[]{:S(2)}) collective-permute-start(bf16[96,3584]{1,0:T(8,128)(2,1)S(1)} %fusion.2), channel_id=1, source_target_pairs={{0,2},{1,3},{2,0},{3,1},{4,6},{5,7},{6,4},{7,5},{8,10},{9,11},{10,... | collective-permute-start | bytes 2064392 | tf_op jit(solution)/shard_map/ppermute | solution.py:206
  73.7 29.6 %collective-permute-start.7 = (bf16[96,3584]{1,0:T(8,128)(2,1)S(1)}, bf16[96,3584]{1,0:T(8,128)(2,1)S(1)}, u32[]{:S(2)}, u32[]{:S(2)}) collective-permute-start(bf16[96,3584]{1,0:T(8,128)(2,1)S(1)} %copy-done.19), channel_id=1, source_target_pairs={{0,2},{1,3},{2,0},{3,1},{4,6},{5,7},{6,4},{7,5},{8,10},{9,11},{10,... | collective-permute-start | bytes 2064392 | tf_op jit(solution)/shard_map/ppermute | solution.py:206
  90.5 14.4 %copy-start.10 = (bf16[96,3584]{1,0:T(8,128)(2,1)}, bf16[96,3584]{1,0:T(8,128)(2,1)S(1)}, u32[]{:S(2)}) copy-start(bf16[96,3584]{1,0:T(8,128)(2,1)S(1)} %collective-permute-done.6) | copy-start | bytes 2064388
  103.3 1.6 copy-start.12
  104.9 2.5 %collective-permute-start.9 = (bf16[96,3584]{1,0:T(8,128)(2,1)}, bf16[96,3584]{1,0:T(8,128)(2,1)}, u32[]{:S(2)}, u32[]{:S(2)}) collective-permute-start(bf16[96,3584]{1,0:T(8,128)(2,1)} %multiply_convert_fusion.2), channel_id=1, source_target_pairs={{0,1},{1,0},{2,3},{3,2},{4,5},{5,4},{6,7},{7,6},{8,9},{9,8},{10,11... | collective-permute-start | bytes 2064392 | tf_op jit(solution)/shard_map/ppermute | solution.py:210
  104.9 18.0 %collective-permute-start.8 = (bf16[96,3584]{1,0:T(8,128)(2,1)}, bf16[96,3584]{1,0:T(8,128)(2,1)S(1)}, u32[]{:S(2)}, u32[]{:S(2)}) collective-permute-start(bf16[96,3584]{1,0:T(8,128)(2,1)} %fusion.6), channel_id=1, source_target_pairs={{0,2},{1,3},{2,0},{3,1},{4,6},{5,7},{6,4},{7,5},{8,10},{9,11},{10,... | collective-permute-start | bytes 2064392 | tf_op jit(solution)/shard_map/ppermute | solution.py:206
  107.4 17.0 %copy-start.4 = (f32[192,3584]{1,0:T(8,128)S(1)}, f32[192,3584]{1,0:T(8,128)}, u32[]{:S(2)}) copy-start(f32[192,3584]{1,0:T(8,128)} %fusion.8) | copy-start | bytes 8257540
  107.4 17.0 %copy-start.6 = (f32[192,3584]{1,0:T(8,128)S(1)}, f32[192,3584]{1,0:T(8,128)}, u32[]{:S(2)}) copy-start(f32[192,3584]{1,0:T(8,128)} %copy-done.5) | copy-start | bytes 8257540
  107.4 17.0 %copy-start.11 = (bf16[96,3584]{1,0:T(8,128)(2,1)S(1)}, bf16[96,3584]{1,0:T(8,128)(2,1)}, u32[]{:S(2)}) copy-start(bf16[96,3584]{1,0:T(8,128)(2,1)} %copy-done.10) | copy-start | bytes 2064388
  107.4 17.0 %copy-start.13 = (bf16[96,3584]{1,0:T(8,128)(2,1)S(1)}, bf16[96,3584]{1,0:T(8,128)(2,1)}, u32[]{:S(2)}) copy-start(bf16[96,3584]{1,0:T(8,128)(2,1)} %copy-done.12) | copy-start | bytes 2064388
  114.7 10.8 %copy-start.17 = (f32[192,2048]{1,0:T(8,128)}, f32[192,2048]{1,0:T(8,128)S(1)}, u32[]{:S(2)}) copy-start(f32[192,2048]{1,0:T(8,128)S(1)} %fusion.7) | copy-start | bytes 4718596
  114.7 9.6 %copy-start.2 = (f32[192,3584]{1,0:T(8,128)S(1)}, f32[192,3584]{1,0:T(8,128)}, u32[]{:S(2)}) copy-start(f32[192,3584]{1,0:T(8,128)} %copy-done) | copy-start | bytes 8257540
  124.4 2.6 %copy-start.15 = (bf16[96,2048]{1,0:T(8,128)(2,1)S(1)}, bf16[96,2048]{1,0:T(8,128)(2,1)}, u32[]{:S(2)}) copy-start(bf16[96,2048]{1,0:T(8,128)(2,1)} %copy-done.14) | copy-start | bytes 1179652
  125.6 10.6 %collective-permute-start.12 = (bf16[96,2048]{1,0:T(8,128)(2,1)S(1)}, bf16[96,2048]{1,0:T(8,128)(2,1)S(1)}, u32[]{:S(2)}, u32[]{:S(2)}) collective-permute-start(bf16[96,2048]{1,0:T(8,128)(2,1)S(1)} %dynamic-slice_convert_fusion.1), channel_id=1, source_target_pairs={{0,4},{4,0},{8,12},{12,8},{16,20},{20,16},{24,28},{28,24},{1,5},{5... | collective-permute-start | bytes 1179656 | tf_op jit(solution)/shard_map/ppermute | solution.py:200
  126.5 9.7 %collective-permute-start.10 = (bf16[96,3584]{1,0:T(8,128)(2,1)S(1)}, bf16[96,3584]{1,0:T(8,128)(2,1)S(1)}, u32[]{:S(2)}, u32[]{:S(2)}) collective-permute-start(bf16[96,3584]{1,0:T(8,128)(2,1)S(1)} %get-tuple-element.53), channel_id=1, source_target_pairs={{0,1},{1,0},{2,3},{3,2},{4,5},{5,4},{6,7},{7,6},{8,9},{9,8},{10,11... | collective-permute-start | bytes 2064392 | tf_op jit(solution)/shard_map/ppermute | solution.py:210
  126.5 9.7 %collective-permute-start.11 = (bf16[96,3584]{1,0:T(8,128)(2,1)S(1)}, bf16[96,3584]{1,0:T(8,128)(2,1)S(1)}, u32[]{:S(2)}, u32[]{:S(2)}) collective-permute-start(bf16[96,3584]{1,0:T(8,128)(2,1)S(1)} %get-tuple-element.54), channel_id=1, source_target_pairs={{0,1},{1,0},{2,3},{3,2},{4,5},{5,4},{6,7},{7,6},{8,9},{9,8},{10,11... | collective-permute-start | bytes 2064392 | tf_op jit(solution)/shard_map/ppermute | solution.py:210
  127.0 9.2 %copy-start.18 = (f32[192,2048]{1,0:T(8,128)S(1)}, f32[192,2048]{1,0:T(8,128)}, u32[]{:S(2)}) copy-start(f32[192,2048]{1,0:T(8,128)} %copy-done.17) | copy-start | bytes 4718596
  136.3 10.8 %collective-permute-start.13 = (bf16[48,2048]{1,0:T(8,128)(2,1)S(1)}, bf16[48,2048]{1,0:T(8,128)(2,1)S(1)}, u32[]{:S(2)}, u32[]{:S(2)}) collective-permute-start(bf16[48,2048]{1,0:T(8,128)(2,1)S(1)} %dynamic-slice_convert_fusion.3), channel_id=1, source_target_pairs={{0,16},{4,20},{8,24},{12,28},{16,0},{20,4},{24,8},{28,12},{1,17},{... | collective-permute-start | bytes 589832 | tf_op jit(solution)/shard_map/ppermute | solution.py:200
  136.5 1.1 copy-start.9
  145.8 10.6 %copy-start.7 = (bf16[192,3584]{1,0:T(8,128)(2,1)}, bf16[192,3584]{1,0:T(8,128)(2,1)S(1)}, u32[]{:S(2)}) copy-start(bf16[192,3584]{1,0:T(8,128)(2,1)S(1)} %pad_maximum_fusion.1.right_ref) | copy-start | bytes 4128772
  147.2 9.4 %collective-permute-start.14 = (bf16[24,2048]{1,0:T(8,128)(2,1)S(1)}, bf16[24,2048]{1,0:T(8,128)(2,1)S(1)}, u32[]{:S(2)}, u32[]{:S(2)}) collective-permute-start(bf16[24,2048]{1,0:T(8,128)(2,1)S(1)} %dynamic-slice_convert_fusion.5), channel_id=1, source_target_pairs={{0,8},{4,12},{8,0},{12,4},{16,24},{20,28},{24,16},{28,20},{1,9},{5... | collective-permute-start | bytes 294920 | tf_op jit(solution)/shard_map/ppermute | solution.py:200
  156.7 10.7 %collective-permute-start.15 = (bf16[96,2048]{1,0:T(8,128)(2,1)S(1)}, bf16[96,2048]{1,0:T(8,128)(2,1)S(1)}, u32[]{:S(2)}, u32[]{:S(2)}) collective-permute-start(bf16[96,2048]{1,0:T(8,128)(2,1)S(1)} %dynamic-slice_convert_fusion), channel_id=1, source_target_pairs={{0,4},{4,0},{8,12},{12,8},{16,20},{20,16},{24,28},{28,24},{1,5},{5... | collective-permute-start | bytes 1179656 | tf_op jit(solution)/shard_map/ppermute | solution.py:200
  167.6 11.5 %collective-permute-start.16 = (bf16[48,2048]{1,0:T(8,128)(2,1)S(1)}, bf16[48,2048]{1,0:T(8,128)(2,1)S(1)}, u32[]{:S(2)}, u32[]{:S(2)}) collective-permute-start(bf16[48,2048]{1,0:T(8,128)(2,1)S(1)} %dynamic-slice_convert_fusion.2), channel_id=1, source_target_pairs={{0,16},{4,20},{8,24},{12,28},{16,0},{20,4},{24,8},{28,12},{1,17},{... | collective-permute-start | bytes 589832 | tf_op jit(solution)/shard_map/ppermute | solution.py:200
  179.1 4.7 %collective-permute-start.17 = (bf16[24,2048]{1,0:T(8,128)(2,1)S(1)}, bf16[24,2048]{1,0:T(8,128)(2,1)S(1)}, u32[]{:S(2)}, u32[]{:S(2)}) collective-permute-start(bf16[24,2048]{1,0:T(8,128)(2,1)S(1)} %dynamic-slice_convert_fusion.4), channel_id=1, source_target_pairs={{0,8},{4,12},{8,0},{12,4},{16,24},{20,28},{24,16},{28,20},{1,9},{5... | collective-permute-start | bytes 294920 | tf_op jit(solution)/shard_map/ppermute | solution.py:200
